TPU v7x, 32 devices: a whole 2x2x4 slice. The times are simulated.
32 devices in a mesh: frames: 2 (over y), az: 8 (over z, x), rg: 2 (over core).
Axes of the slice: x: 2, y: 2, z: 4, core: 2. Of those that a mesh axis runs over, the one named last changes fastest.
Arguments:
- raw: bfloat16 [2, 512, 8, 2048], P(None, ('frames', 'az'), None, 'rg'), parts along dimension 1, may hold values from -6 to 6
- stolt_weights: bfloat16 [4, 16, 256, 128], P(None, 'rg'), may hold values from -0.375 to 0.375
- band_start: int32 [4, 16], replicated, may hold values from 0 to 14, as said below
Outputs:
- image: bfloat16 [2, 512, 8, 2048], P(None, ('frames', 'az'), None, 'rg'), parts along dimension 1
There are 2 independent parts, one for each index of `frames`. A program takes and returns all parts, laid end to end along the dimension named above; an argument that names none is the same for every part. Nothing has to cross between parts.
Inputs may be any that keep to these rules, and one draw needn't show every extreme that they name: band_start[g, j] is (j) - 1 or (j), clipped to the range; for every block j from 1 to 14 some slab has (j) - 1 and some slab has (j).
All inputs are finite; a program needn't handle non-finite values.
Results may differ from a plain program's by a relative error of at most 0.001.
Values may be sent and summed in bfloat16 or wider, within the bound.
No kernel may reach another device: no remote copies, remote signals or barrier semaphores. Data moves between devices by JAX's collectives and lax.ppermute only.
A program may use at most 64 MiB of HBM per device.

v0:
```python
import math
import jax
import jax.numpy as jnp
from jax import lax
from jax.sharding import PartitionSpec as P

LINES_DEV = 256
SLABS = 4


def with_halo(cells, sides, width):
    for axis, dim in sides:
        count = lax.axis_size(axis)
        ends = count - 1
        head = lax.slice_in_dim(cells, 0, width, axis=dim)
        tail = lax.slice_in_dim(cells, cells.shape[dim] - width, cells.shape[dim], axis=dim)
        cells = jnp.concatenate(
            [
                lax.ppermute(tail, axis, [(i, (i + 1) % count) for i in range(ends)]),
                cells,
                lax.ppermute(head, axis, [((i + 1) % count, i) for i in range(ends)]),
            ],
            axis=dim,
        )
    return cells


def dft_table(length, direction, factor):
    counter = jnp.arange(length, dtype=jnp.int32)
    product = counter[:, None] * counter[None, :] % length
    angles = product.astype(jnp.float32) * (2.0 * math.pi / length)
    cosine = jnp.cos(angles) * factor
    sines = jnp.sin(angles) * (factor * direction)
    return jnp.stack([jnp.stack([cosine, -sines], 1), jnp.stack([sines, cosine], 1)], 0)


def rotate(real_part, imag_part, phase_index, line_total, direction):
    angles = phase_index.astype(jnp.float32) * (2.0 * math.pi / line_total)
    cosine = jnp.cos(angles)
    sines = jnp.sin(angles) * direction
    return (real_part * cosine - imag_part * sines, imag_part * cosine + real_part * sines)


def stolt(slab_source, weights, starts, slab_rows):
    pieces = []
    for slab_index in range(weights.shape[0]):
        slab_data = slab_source[:, slab_index * slab_rows : (slab_index + 1) * slab_rows, :]

        def window_at(start_bin):
            return lax.dynamic_slice_in_dim(slab_data, start_bin, 256, 2)

        windows = jax.vmap(window_at)(starts[slab_index])
        remixed = jnp.einsum(
            "jcmb,jbo->cmjo",
            windows,
            weights[slab_index].astype(jnp.float32),
            precision=lax.Precision.HIGHEST,
        )
        pieces.append(remixed.reshape(2, slab_rows, -1))
    return jnp.concatenate(pieces, 1)


def body(raw, stolt_weights, band_start):
    groups = lax.axis_size("az")
    az_index = lax.axis_index("az")
    rg_index = lax.axis_index("rg")
    part_lines = raw.shape[1]
    bin_count = raw.shape[3]
    line_total = LINES_DEV * groups
    short_forward = dft_table(groups, -1.0, 1.0 / math.sqrt(groups))
    spread = jnp.einsum(
        "dkcp,cmpr->dmkr", short_forward, raw.astype(jnp.float32), precision=lax.Precision.HIGHEST
    )
    line_index = az_index * part_lines + jnp.arange(part_lines, dtype=jnp.int32)
    freq_index = jnp.arange(groups, dtype=jnp.int32)
    phase_index = line_index[:, None] * freq_index[None, :] % line_total
    real_part, imag_part = rotate(spread[0], spread[1], phase_index[:, :, None], line_total, -1.0)
    twisted = jnp.stack([real_part, imag_part])
    long_forward = dft_table(LINES_DEV, -1.0, 1.0 / math.sqrt(LINES_DEV))
    spectrum = jnp.einsum(
        "dkcm,cmjr->dkjr",
        long_forward,
        lax.all_to_all(twisted, "az", split_axis=2, concat_axis=1, tiled=True),
        precision=lax.Precision.HIGHEST,
    )
    spectrum_rows = spectrum[:, :, 0, :]
    slab_rows = LINES_DEV // SLABS
    block_count = bin_count // 128
    padded = with_halo(spectrum_rows, (("rg", 2),), 128)
    local_band = lax.dynamic_slice_in_dim(band_start, rg_index * block_count, block_count, 1)
    starts = (local_band - rg_index * block_count) * 128 + 128
    remapped = stolt(padded, stolt_weights, starts, slab_rows)
    long_inverse = dft_table(LINES_DEV, 1.0, 1.0 / math.sqrt(LINES_DEV))
    lines_back = jnp.einsum(
        "dmck,ckr->dmr", long_inverse, remapped, precision=lax.Precision.HIGHEST
    )
    all_lines = jnp.arange(LINES_DEV, dtype=jnp.int32)
    back_index = all_lines * az_index % line_total
    real_part, imag_part = rotate(
        lines_back[0], lines_back[1], back_index[:, None], line_total, 1.0
    )
    unrolled = jnp.stack([real_part, imag_part])[:, :, None, :]
    short_inverse = dft_table(groups, 1.0, 1.0 / math.sqrt(groups))
    focused = jnp.einsum(
        "dpck,cmkr->dmpr",
        short_inverse,
        lax.all_to_all(unrolled, "az", split_axis=1, concat_axis=2, tiled=True),
        precision=lax.Precision.HIGHEST,
    )
    return focused.astype(jnp.bfloat16)


def solution(mesh):
    placed = (P(None, ("frames", "az"), None, "rg"), P(None, "rg", None, None), P())
    return jax.shard_map(
        body,
        mesh=mesh,
        in_specs=placed,
        out_specs=P(None, ("frames", "az"), None, "rg"),
        check_vma=False,
    )
```

profile of v0, /device:TPU:0, one launch (start us, length us, event | category | flops | bytes accessed | tf_op | source)
XLA Modules:
  0.0 164.7 jit_solution(4455382401302081138)
XLA Ops:
  0.0 0.1 cosine_multiply_fusion.1
  0.1 0.1 broadcast_multiply_fusion.3
  0.1 0.1 fusion.88
  0.2 0.2 fusion.79
  0.4 2.3 %convolution_bitcast_fusion.1 = f32[2,32,8,1024]{3,2,1,0:T(8,128)S(1)} fusion(bf16[2,32,8,1024]{3,2,1,0:T(8,128)(2,1)} %param.3, f32[1,8,2,8]{3,1,2,0:T(8,128)S(1)} %get-tuple-element.21, f32[1,8,2,8]{3,1,2,0:T(8,128)S(1)} %get-tuple-element.22), kind=kOutput, calls=%fused_computation.29 | convolution fusion | flops 100663552 | bytes 3146752 | tf_op jit(solution)/shard_map/dkcp,cmpr->dmkr/dot_general | solution.py:71
  2.6 0.3 multiply_subtract_fusion.1
  2.9 0.2 pad_maximum_fusion.1
  3.2 2.6 %copy.49 = f32[2,32,8,1024]{3,1,0,2:T(8,128)} copy(f32[2,32,8,1024]{3,2,1,0:T(8,128)S(1)} %pad_maximum_fusion.1) | data formatting | bytes 4194304 | tf_op jit(solution)/shard_map/stack | solution.py:78
  5.7 7.3 %all-to-all-start = ((f32[2,32,8,1024]{3,1,0,2:T(8,128)}), f32[2,32,8,1024]{3,1,0,2:T(8,128)S(1)}, u32[]{:S(2)}, u32[]{:S(2)}) async-start(f32[2,32,8,1024]{3,1,0,2:T(8,128)} %copy.49), calls=%async_computation | async-start | bytes 4194304 | tf_op jit(solution)/shard_map/all_to_all | solution.py:83
  13.0 0.1 fusion.104
  13.0 1.0 fusion.64
  14.0 1.1 cosine_multiply_fusion
  15.1 1.0 broadcast_multiply_fusion.1
  16.1 1.2 fusion.46
  17.2 44.0 %all-to-all-done = f32[2,32,8,1024]{3,1,0,2:T(8,128)S(1)} async-done(((f32[2,32,8,1024]{3,1,0,2:T(8,128)}), f32[2,32,8,1024]{3,1,0,2:T(8,128)S(1)}, u32[]{:S(2)}, u32[]{:S(2)}) %all-to-all-start) | async-done | bytes 2097184 | tf_op jit(solution)/shard_map/all_to_all | solution.py:83
  61.2 0.1 copy.50
  61.4 0.0 copy-start.5
  61.4 3.6 %convolution_bitcast_fusion = f32[2,256,1024]{2,1,0:T(8,128)S(1)} fusion(f32[2,256,1024,1]{2,1,0,3:T(8,128)S(1)} %bitcast.139, f32[1,256,2,256]{3,1,2,0:T(8,128)S(1)} %get-tuple-element.16, f32[1,256,2,256]{3,1,2,0:T(8,128)S(1)} %get-tuple-element.17), kind=kOutput, calls=%fused_computation.28 | convolution fusion | flops 3221487616 | bytes 5242880 | tf_op jit(solution)/shard_map/dkcm,cmjr->dkjr/dot_general | solution.py:80
  65.0 1.3 collective-permute-start
  66.3 1.3 collective-permute-start.1
  67.6 0.1 multiply_add_fusion.2
  67.7 0.0 collective-permute-done
  67.8 2.0 %collective-permute-done.1 = f32[2,256,128]{2,1,0:T(8,128)S(1)} collective-permute-done((f32[2,256,128]{2,1,0:T(8,128)S(1)}, f32[2,256,128]{2,1,0:T(8,128)S(1)}, u32[]{:S(2)}, u32[]{:S(2)}) %collective-permute-start.1) | collective-permute-done | bytes 262176 | tf_op jit(solution)/shard_map/ppermute | solution.py:21
  69.8 0.2 pad_maximum_fusion
  70.0 1.3 fusion.110
  71.3 0.7 copy.57
  71.9 2.8 %gather_fusion.2 = f32[8,2,64,256]{2,1,3,0:T(2,128)S(1)} fusion(f32[2,64,1280]{1,0,2:T(2,128)S(1)} %copy.57, s32[8]{0:T(128)S(1)} %get-tuple-element.25), kind=kCustom, calls=%fused_computation.2 | custom fusion | bytes 2097248 | tf_op jit(solution)/shard_map/vmap()/gather | solution.py:50
  74.7 2.9 %fusion.30 = f32[8,2,8,8,128]{4,3,2,1,0:T(8,128)S(1)} fusion(f32[8,2,64,256]{2,1,3,0:T(2,128)S(1)} %gather_fusion.2, bf16[4,8,256,128]{3,2,1,0:T(8,128)(2,1)} %param.4), kind=kOutput, calls=%fused_computation.33 | convolution fusion | flops 402653184 | bytes 2097152 | tf_op jit(solution)/shard_map/jcmb,jbo->cmjo/dot_general | solution.py:53
  77.6 0.9 copy.116
  78.5 1.6 copy.54
  80.1 2.8 %gather_fusion.1 = f32[8,2,64,256]{2,1,3,0:T(2,128)S(1)} fusion(f32[2,64,1280]{1,0,2:T(2,128)S(1)} %copy.54, s32[8]{0:T(128)S(1)} %get-tuple-element.26), kind=kCustom, calls=%fused_computation.1 | custom fusion | bytes 2097248 | tf_op jit(solution)/shard_map/vmap()/gather | solution.py:50
  82.9 2.9 %fusion.27 = f32[8,2,8,8,128]{4,3,2,1,0:T(8,128)S(1)} fusion(f32[8,2,64,256]{2,1,3,0:T(2,128)S(1)} %gather_fusion.1, bf16[4,8,256,128]{3,2,1,0:T(8,128)(2,1)} %param.4), kind=kOutput, calls=%fused_computation.32 | convolution fusion | flops 402653184 | bytes 2097152 | tf_op jit(solution)/shard_map/jcmb,jbo->cmjo/dot_general | solution.py:53
  85.8 0.9 copy.117
  86.6 1.6 copy.51
  88.2 2.8 %gather_fusion = f32[8,2,64,256]{2,1,3,0:T(2,128)S(1)} fusion(f32[2,64,1280]{1,0,2:T(2,128)S(1)} %copy.51, s32[8]{0:T(128)S(1)} %get-tuple-element.23), kind=kCustom, calls=%fused_computation | custom fusion | bytes 2097248 | tf_op jit(solution)/shard_map/vmap()/gather | solution.py:50
  91.0 2.9 %fusion.24 = f32[8,2,8,8,128]{4,3,2,1,0:T(8,128)S(1)} fusion(f32[8,2,64,256]{2,1,3,0:T(2,128)S(1)} %gather_fusion, bf16[4,8,256,128]{3,2,1,0:T(8,128)(2,1)} %param.4), kind=kOutput, calls=%fused_computation.31 | convolution fusion | flops 402653184 | bytes 2097152 | tf_op jit(solution)/shard_map/jcmb,jbo->cmjo/dot_general | solution.py:53
  93.9 0.9 copy.118
  94.7 1.6 copy.60
  96.3 2.8 %gather_fusion.3 = f32[8,2,64,256]{2,1,3,0:T(2,128)S(1)} fusion(f32[2,64,1280]{1,0,2:T(2,128)S(1)} %copy.60, s32[8]{0:T(128)S(1)} %get-tuple-element.24), kind=kCustom, calls=%fused_computation.3 | custom fusion | bytes 2097248 | tf_op jit(solution)/shard_map/vmap()/gather | solution.py:50
  99.1 0.0 copy-start.2
  99.2 3.0 %fusion.33 = f32[8,2,8,8,128]{4,3,2,1,0:T(8,128)S(1)} fusion(f32[8,2,64,256]{2,1,3,0:T(2,128)S(1)} %gather_fusion.3, bf16[4,8,256,128]{3,2,1,0:T(8,128)(2,1)} %param.4), kind=kOutput, calls=%fused_computation.34 | convolution fusion | flops 402653184 | bytes 2097152 | tf_op jit(solution)/shard_map/jcmb,jbo->cmjo/dot_general | solution.py:53
  102.3 3.6 %fusion.18 = f32[2,256,1024]{2,1,0:T(8,128)S(1)} fusion(f32[2,64,1024]{2,1,0:T(8,128)S(1)} %bitcast.143, f32[2,64,1024]{2,1,0:T(8,128)S(1)} %bitcast.140, f32[2,64,1024]{2,1,0:T(8,128)S(1)} %bitcast.141, f32[2,64,1024]{2,1,0:T(8,128)S(1)} %bitcast.142, f32[1,256,2,256]{3,1,2,0:T(8,128)S(1)} %copy-done.4, f32[1,256,2,256]{3,1,2,0:T(8,128)S(1)} %copy-done.3), kind=kOutput, calls=%fused_computation.27 | convolution fusion | flops 3223060480 | bytes 5242880 | tf_op jit(solution)/shard_map/dmck,ckr->dmr/dot_general | solution.py:94
  105.9 0.3 multiply_subtract_fusion
  106.2 0.2 maximum_bitcast_fusion.2
  106.5 1.6 copy.63
  108.1 52.6 %all_to_all.33 = f32[2,256,1,1024]{3,0,2,1:T(2,128)S(1)} all-to-all(f32[2,256,1,1024]{3,0,2,1:T(2,128)S(1)} %copy.63), channel_id=1, replica_groups=mesh['frames'=2,'az'=8,'rg'=2] {'az'}, dimensions={1} | all-to-all | bytes 4194304 | tf_op jit(solution)/shard_map/all_to_all | solution.py:107
  160.6 3.0 %fusion.21 = bf16[2,32,8,1024]{3,2,0,1:T(8,128)(2,1)S(1)} fusion(f32[2,8,32,1,1024]{4,0,2,1,3:T(2,128)S(1)} %bitcast.138, f32[1,8,2,8]{3,1,2,0:T(8,128)S(1)} %get-tuple-element.20, f32[1,8,2,8]{3,1,2,0:T(8,128)S(1)} %get-tuple-element.19), kind=kOutput, calls=%fused_computation.30 | convolution fusion | flops 101187840 | bytes 3146752 | tf_op jit(solution)/shard_map/dpck,cmkr->dmpr/dot_general | solution.py:104
  163.6 1.1 copy.66
  (15 shorter events, 0.1 us)
Async XLA Ops:
  5.7 55.5 %all-to-all-start = ((f32[2,32,8,1024]{3,1,0,2:T(8,128)}), f32[2,32,8,1024]{3,1,0,2:T(8,128)S(1)}, u32[]{:S(2)}, u32[]{:S(2)}) async-start(f32[2,32,8,1024]{3,1,0,2:T(8,128)} %copy.49), calls=%async_computation | async-start | bytes 4194304 | tf_op jit(solution)/shard_map/all_to_all | solution.py:83
  61.4 6.3 %copy-start.5 = (s32[4,16]{1,0:T(4,128)S(1)}, s32[4,16]{1,0:T(4,128)}, u32[]{:S(2)}) copy-start(s32[4,16]{1,0:T(4,128)} %param.5) | copy-start | bytes 772
  65.0 2.7 %collective-permute-start = (f32[2,256,128]{2,1,0:T(8,128)S(1)}, f32[2,256,128]{2,1,0:T(8,128)S(1)}, u32[]{:S(2)}, u32[]{:S(2)}) collective-permute-start(f32[2,256,128]{2,1,0:T(8,128)S(1)} %get-tuple-element.13), channel_id=1, source_target_pairs={{0,1},{2,3},{4,5},{6,7},{8,9},{10,11},{12,13},{14,15},{16,17},{18,... | collective-permute-start | bytes 786440 | tf_op jit(solution)/shard_map/ppermute | solution.py:19
  66.3 3.4 %collective-permute-start.1 = (f32[2,256,128]{2,1,0:T(8,128)S(1)}, f32[2,256,128]{2,1,0:T(8,128)S(1)}, u32[]{:S(2)}, u32[]{:S(2)}) collective-permute-start(f32[2,256,128]{2,1,0:T(8,128)S(1)} %get-tuple-element.14), channel_id=1, source_target_pairs={{1,0},{3,2},{5,4},{7,6},{9,8},{11,10},{13,12},{15,14},{17,16},{19,... | collective-permute-start | bytes 786440 | tf_op jit(solution)/shard_map/ppermute | solution.py:21
  99.1 3.1 %copy-start = (f32[8,2,8,8,128]{4,3,0,2,1:T(8,128)S(1)}, f32[8,2,8,8,128]{4,3,0,2,1:T(8,128)}, u32[]{:S(2)}) copy-start(f32[8,2,8,8,128]{4,3,0,2,1:T(8,128)} %copy.116) | copy-start | bytes 1572868
  99.1 3.1 %copy-start.1 = (f32[8,2,8,8,128]{4,3,0,2,1:T(8,128)S(1)}, f32[8,2,8,8,128]{4,3,0,2,1:T(8,128)}, u32[]{:S(2)}) copy-start(f32[8,2,8,8,128]{4,3,0,2,1:T(8,128)} %copy.117) | copy-start | bytes 1572868
  99.1 3.1 %copy-start.2 = (f32[8,2,8,8,128]{4,3,0,2,1:T(8,128)S(1)}, f32[8,2,8,8,128]{4,3,0,2,1:T(8,128)}, u32[]{:S(2)}) copy-start(f32[8,2,8,8,128]{4,3,0,2,1:T(8,128)} %copy.118) | copy-start | bytes 1572868
  99.1 3.1 %copy-start.3 = (f32[1,256,2,256]{3,1,2,0:T(8,128)S(1)}, f32[1,256,2,256]{3,1,2,0:T(8,128)}, u32[]{:S(2)}) copy-start(f32[1,256,2,256]{3,1,2,0:T(8,128)} %get-tuple-element.15) | copy-start | bytes 1572868
  99.2 3.1 %copy-start.4 = (f32[1,256,2,256]{3,1,2,0:T(8,128)S(1)}, f32[1,256,2,256]{3,1,2,0:T(8,128)}, u32[]{:S(2)}) copy-start(f32[1,256,2,256]{3,1,2,0:T(8,128)} %get-tuple-element.18) | copy-start | bytes 1572868
where the time goes:
time: 165 us
  blocking collectives  52.6 us (32%)
  waiting for transfers between devices  46 us (28%)
  local copies, waits for them, and re-layouts  25.9 us (16%)
  matrix products  24.1 us (15%)
  starting transfers between devices  9.85 us (6%)
  other arithmetic  5.92 us (4%)
    all_to_all x1, blocking collectives, body(): lax.all_to_all(unrolled, 'az', split_axis=1, concat_axis=2, tiled=True)  52.6 us
    all_to_all x1, waiting for transfers between devices, body(): lax.all_to_all(twisted, 'az', split_axis=2, concat_axis=1, tiled=True)  44 us
    dot_general x4, matrix products, stolt(): jnp.einsum('jcmb,jbo->cmjo', windows, weights[slab_index].astype(jnp.floa...  11.7 us
    gather x4, local copies, waits for them, and re-layouts, window_at(): return lax.dynamic_slice_in_dim(slab_data, start_bin, 256, 2)  11.2 us
    all_to_all x1, starting transfers between devices, body(): lax.all_to_all(twisted, 'az', split_axis=2, concat_axis=1, tiled=True)  7.25 us
    slice x5, local copies, waits for them, and re-layouts, stolt(): slab_source[:, slab_index * slab_rows:(slab_index + 1) * slab_rows, :]  6.67 us
    dot_general x1, matrix products, body(): jnp.einsum('dkcm,cmjr->dkjr', long_forward, lax.all_to_all(twisted, 'az',...  3.58 us
    dot_general x1, matrix products, body(): jnp.einsum('dmck,ckr->dmr', long_inverse, remapped, precision=lax.Precisi...  3.58 us
  transfers between devices with their start and end apart: 3, of which 2 were waited for; matrix products, arithmetic and copies ran while one was open for 3% of the time, Pallas kernels for 0%

commit v1 on v0

--- a/solution.py
+++ b/solution.py
@@ -6,6 +6,12 @@
 
 LINES_DEV = 256
 SLABS = 4
+
+
+def track_region(field_in):
+    part_now = jnp.stack(jnp.split(field_in, lax.axis_size("az"), axis=1))
+    carry_in = lax.all_to_all(part_now, axis_name="az", split_axis=0, concat_axis=0)
+    return jnp.concatenate(carry_in, axis=2)
 
 
 def with_halo(cells, sides, width):
@@ -102,10 +108,7 @@
     unrolled = jnp.stack([real_part, imag_part])[:, :, None, :]
     short_inverse = dft_table(groups, 1.0, 1.0 / math.sqrt(groups))
     focused = jnp.einsum(
-        "dpck,cmkr->dmpr",
-        short_inverse,
-        lax.all_to_all(unrolled, "az", split_axis=1, concat_axis=2, tiled=True),
-        precision=lax.Precision.HIGHEST,
+        "dpck,cmkr->dmpr", short_inverse, track_region(unrolled), precision=lax.Precision.HIGHEST
     )
     return focused.astype(jnp.bfloat16)
 

time: 165 us -> 164 us (level)
  no operation moved by 1% of the time
where the time goes in v1:
time: 164 us; the launch traced here: 163 us
  blocking collectives  52.6 us (32%)
  waiting for transfers between devices  46 us (28%)
  local copies, waits for them, and re-layouts  24.4 us (15%)
  matrix products  24.2 us (15%)
  starting transfers between devices  9.85 us (6%)
  other arithmetic  5.93 us (4%)
    all_to_all x1, blocking collectives, track_region(): lax.all_to_all(part_now, axis_name='az', split_axis=0, concat_axis=0)  52.6 us
    all_to_all x1, waiting for transfers between devices, body(): lax.all_to_all(twisted, 'az', split_axis=2, concat_axis=1, tiled=True)  44 us
    dot_general x4, matrix products, stolt(): jnp.einsum('jcmb,jbo->cmjo', windows, weights[slab_index].astype(jnp.floa...  11.7 us
    gather x4, local copies, waits for them, and re-layouts, window_at(): return lax.dynamic_slice_in_dim(slab_data, start_bin, 256, 2)  11.2 us
    all_to_all x1, starting transfers between devices, body(): lax.all_to_all(twisted, 'az', split_axis=2, concat_axis=1, tiled=True)  7.25 us
    slice x5, local copies, waits for them, and re-layouts, stolt(): slab_source[:, slab_index * slab_rows:(slab_index + 1) * slab_rows, :]  6.67 us
    dot_general x1, matrix products, body(): jnp.einsum('dkcm,cmjr->dkjr', long_forward, lax.all_to_all(twisted, 'az',...  3.58 us
    dot_general x1, matrix products, body(): jnp.einsum('dmck,ckr->dmr', long_inverse, remapped, precision=lax.Precisi...  3.58 us
  transfers between devices with their start and end apart: 3, of which 2 were waited for; matrix products, arithmetic and copies ran while one was open for 3% of the time, Pallas kernels for 0%

profile of v1, /device:TPU:0, one launch (start us, length us, event | category | flops | bytes accessed | tf_op | source)
XLA Modules:
  0.0 163.4 jit_solution(396282825998567294)
XLA Ops:
  0.0 0.1 cosine_multiply_fusion.1
  0.1 0.1 broadcast_multiply_fusion.3
  0.1 0.1 fusion.95
  0.2 0.2 fusion.86
  0.4 2.3 %convolution_bitcast_fusion.1 = f32[2,32,8,1024]{3,2,1,0:T(8,128)S(1)} fusion(bf16[2,32,8,1024]{3,2,1,0:T(8,128)(2,1)} %param.3, f32[1,8,2,8]{3,1,2,0:T(8,128)S(1)} %get-tuple-element.21, f32[1,8,2,8]{3,1,2,0:T(8,128)S(1)} %get-tuple-element.22), kind=kOutput, calls=%fused_computation.28 | convolution fusion | flops 100663552 | bytes 3146752 | tf_op jit(solution)/shard_map/dkcp,cmpr->dmkr/dot_general | solution.py:77
  2.6 0.3 multiply_subtract_fusion.1
  2.9 0.2 pad_maximum_fusion.1
  3.2 2.6 %copy.32 = f32[2,32,8,1024]{3,1,0,2:T(8,128)} copy(f32[2,32,8,1024]{3,2,1,0:T(8,128)S(1)} %pad_maximum_fusion.1) | data formatting | bytes 4194304 | tf_op jit(solution)/shard_map/stack | solution.py:84
  5.7 7.3 %all-to-all-start = ((f32[2,32,8,1024]{3,1,0,2:T(8,128)}), f32[2,32,8,1024]{3,1,0,2:T(8,128)S(1)}, u32[]{:S(2)}, u32[]{:S(2)}) async-start(f32[2,32,8,1024]{3,1,0,2:T(8,128)} %copy.32), calls=%async_computation | async-start | bytes 4194304 | tf_op jit(solution)/shard_map/all_to_all | solution.py:89
  13.0 0.1 fusion.111
  13.0 1.0 fusion.71
  14.0 1.1 cosine_multiply_fusion
  15.1 1.0 broadcast_multiply_fusion.1
  16.1 1.2 fusion.45
  17.2 44.0 %all-to-all-done = f32[2,32,8,1024]{3,1,0,2:T(8,128)S(1)} async-done(((f32[2,32,8,1024]{3,1,0,2:T(8,128)}), f32[2,32,8,1024]{3,1,0,2:T(8,128)S(1)}, u32[]{:S(2)}, u32[]{:S(2)}) %all-to-all-start) | async-done | bytes 2097184 | tf_op jit(solution)/shard_map/all_to_all | solution.py:89
  61.2 0.1 copy.33
  61.4 0.0 copy-start.5
  61.4 3.6 %convolution_bitcast_fusion = f32[2,256,1024]{2,1,0:T(8,128)S(1)} fusion(f32[2,256,1024,1]{2,1,0,3:T(8,128)S(1)} %bitcast.162, f32[1,256,2,256]{3,1,2,0:T(8,128)S(1)} %get-tuple-element.16, f32[1,256,2,256]{3,1,2,0:T(8,128)S(1)} %get-tuple-element.17), kind=kOutput, calls=%fused_computation.27 | convolution fusion | flops 3221487616 | bytes 5242880 | tf_op jit(solution)/shard_map/dkcm,cmjr->dkjr/dot_general | solution.py:86
  65.0 1.3 collective-permute-start
  66.3 1.3 collective-permute-start.1
  67.6 0.1 multiply_add_fusion.2
  67.7 0.0 collective-permute-done
  67.8 2.0 %collective-permute-done.1 = f32[2,256,128]{2,1,0:T(8,128)S(1)} collective-permute-done((f32[2,256,128]{2,1,0:T(8,128)S(1)}, f32[2,256,128]{2,1,0:T(8,128)S(1)}, u32[]{:S(2)}, u32[]{:S(2)}) %collective-permute-start.1) | collective-permute-done | bytes 262176 | tf_op jit(solution)/shard_map/ppermute | solution.py:27
  69.8 0.2 pad_maximum_fusion
  70.0 1.3 fusion.117
  71.3 0.7 copy.40
  71.9 2.8 %gather_fusion.2 = f32[8,2,64,256]{2,1,3,0:T(2,128)S(1)} fusion(f32[2,64,1280]{1,0,2:T(2,128)S(1)} %copy.40, s32[8]{0:T(128)S(1)} %get-tuple-element.25), kind=kCustom, calls=%fused_computation.2 | custom fusion | bytes 2097248 | tf_op jit(solution)/shard_map/vmap()/gather | solution.py:56
  74.7 2.9 %fusion.29 = f32[8,2,8,8,128]{4,3,2,1,0:T(8,128)S(1)} fusion(f32[8,2,64,256]{2,1,3,0:T(2,128)S(1)} %gather_fusion.2, bf16[4,8,256,128]{3,2,1,0:T(8,128)(2,1)} %param.4), kind=kOutput, calls=%fused_computation.32 | convolution fusion | flops 402653184 | bytes 2097152 | tf_op jit(solution)/shard_map/jcmb,jbo->cmjo/dot_general | solution.py:59
  77.6 0.9 copy.95
  78.5 1.6 copy.37
  80.1 2.8 %gather_fusion.1 = f32[8,2,64,256]{2,1,3,0:T(2,128)S(1)} fusion(f32[2,64,1280]{1,0,2:T(2,128)S(1)} %copy.37, s32[8]{0:T(128)S(1)} %get-tuple-element.26), kind=kCustom, calls=%fused_computation.1 | custom fusion | bytes 2097248 | tf_op jit(solution)/shard_map/vmap()/gather | solution.py:56
  82.9 2.9 %fusion.26 = f32[8,2,8,8,128]{4,3,2,1,0:T(8,128)S(1)} fusion(f32[8,2,64,256]{2,1,3,0:T(2,128)S(1)} %gather_fusion.1, bf16[4,8,256,128]{3,2,1,0:T(8,128)(2,1)} %param.4), kind=kOutput, calls=%fused_computation.31 | convolution fusion | flops 402653184 | bytes 2097152 | tf_op jit(solution)/shard_map/jcmb,jbo->cmjo/dot_general | solution.py:59
  85.8 0.9 copy.96
  86.6 1.6 copy.34
  88.2 2.8 %gather_fusion = f32[8,2,64,256]{2,1,3,0:T(2,128)S(1)} fusion(f32[2,64,1280]{1,0,2:T(2,128)S(1)} %copy.34, s32[8]{0:T(128)S(1)} %get-tuple-element.23), kind=kCustom, calls=%fused_computation | custom fusion | bytes 2097248 | tf_op jit(solution)/shard_map/vmap()/gather | solution.py:56
  91.0 2.9 %fusion.23 = f32[8,2,8,8,128]{4,3,2,1,0:T(8,128)S(1)} fusion(f32[8,2,64,256]{2,1,3,0:T(2,128)S(1)} %gather_fusion, bf16[4,8,256,128]{3,2,1,0:T(8,128)(2,1)} %param.4), kind=kOutput, calls=%fused_computation.30 | convolution fusion | flops 402653184 | bytes 2097152 | tf_op jit(solution)/shard_map/jcmb,jbo->cmjo/dot_general | solution.py:59
  93.9 0.9 copy.97
  94.7 1.6 copy.43
  96.3 2.8 %gather_fusion.3 = f32[8,2,64,256]{2,1,3,0:T(2,128)S(1)} fusion(f32[2,64,1280]{1,0,2:T(2,128)S(1)} %copy.43, s32[8]{0:T(128)S(1)} %get-tuple-element.24), kind=kCustom, calls=%fused_computation.3 | custom fusion | bytes 2097248 | tf_op jit(solution)/shard_map/vmap()/gather | solution.py:56
  99.1 0.0 copy-start.2
  99.2 3.0 %fusion.32 = f32[8,2,8,8,128]{4,3,2,1,0:T(8,128)S(1)} fusion(f32[8,2,64,256]{2,1,3,0:T(2,128)S(1)} %gather_fusion.3, bf16[4,8,256,128]{3,2,1,0:T(8,128)(2,1)} %param.4), kind=kOutput, calls=%fused_computation.33 | convolution fusion | flops 402653184 | bytes 2097152 | tf_op jit(solution)/shard_map/jcmb,jbo->cmjo/dot_general | solution.py:59
  102.3 0.0 copy-done
  102.3 3.6 %fusion.17 = f32[2,256,1024]{2,1,0:T(8,128)S(1)} fusion(f32[2,64,1024]{2,1,0:T(8,128)S(1)} %bitcast.166, f32[2,64,1024]{2,1,0:T(8,128)S(1)} %bitcast.163, f32[2,64,1024]{2,1,0:T(8,128)S(1)} %bitcast.164, f32[2,64,1024]{2,1,0:T(8,128)S(1)} %bitcast.165, f32[1,256,2,256]{3,1,2,0:T(8,128)S(1)} %copy-done.4, f32[1,256,2,256]{3,1,2,0:T(8,128)S(1)} %copy-done.3), kind=kOutput, calls=%fused_computation.26 | convolution fusion | flops 3223060480 | bytes 5242880 | tf_op jit(solution)/shard_map/dmck,ckr->dmr/dot_general | solution.py:100
  105.9 0.3 multiply_subtract_fusion
  106.2 0.2 maximum_bitcast_fusion.2
  106.7 52.6 %all_to_all.20 = f32[8,2,32,1,1024]{4,2,1,3,0:T(8,128)S(1)} all-to-all(f32[8,2,32,1,1024]{4,2,1,3,0:T(8,128)S(1)} %fusion.58), channel_id=1, replica_groups=mesh['frames'=2,'az'=8,'rg'=2] {'az'}, dimensions={0} | all-to-all | bytes 4194304 | tf_op jit(solution)/shard_map/all_to_all | solution.py:13
  159.2 3.1 %fusion.20 = bf16[2,32,8,1024]{3,2,0,1:T(8,128)(2,1)S(1)} fusion(f32[2,32,8,1024,1]{3,1,0,2,4:T(8,128)S(1)} %bitcast.161, f32[1,8,2,8]{3,1,2,0:T(8,128)S(1)} %get-tuple-element.20, f32[1,8,2,8]{3,1,2,0:T(8,128)S(1)} %get-tuple-element.19), kind=kOutput, calls=%fused_computation.29 | convolution fusion | flops 101187840 | bytes 3146752 | tf_op jit(solution)/shard_map/dpck,cmkr->dmpr/dot_general | solution.py:110
  162.3 1.1 copy.47
  (22 shorter events, 0.3 us)
Async XLA Ops:
  5.7 55.5 %all-to-all-start = ((f32[2,32,8,1024]{3,1,0,2:T(8,128)}), f32[2,32,8,1024]{3,1,0,2:T(8,128)S(1)}, u32[]{:S(2)}, u32[]{:S(2)}) async-start(f32[2,32,8,1024]{3,1,0,2:T(8,128)} %copy.32), calls=%async_computation | async-start | bytes 4194304 | tf_op jit(solution)/shard_map/all_to_all | solution.py:89
  61.4 6.3 %copy-start.5 = (s32[4,16]{1,0:T(4,128)S(1)}, s32[4,16]{1,0:T(4,128)}, u32[]{:S(2)}) copy-start(s32[4,16]{1,0:T(4,128)} %param.5) | copy-start | bytes 772
  65.0 2.7 %collective-permute-start = (f32[2,256,128]{2,1,0:T(8,128)S(1)}, f32[2,256,128]{2,1,0:T(8,128)S(1)}, u32[]{:S(2)}, u32[]{:S(2)}) collective-permute-start(f32[2,256,128]{2,1,0:T(8,128)S(1)} %get-tuple-element.13), channel_id=1, source_target_pairs={{0,1},{2,3},{4,5},{6,7},{8,9},{10,11},{12,13},{14,15},{16,17},{18,... | collective-permute-start | bytes 786440 | tf_op jit(solution)/shard_map/ppermute | solution.py:25
  66.3 3.4 %collective-permute-start.1 = (f32[2,256,128]{2,1,0:T(8,128)S(1)}, f32[2,256,128]{2,1,0:T(8,128)S(1)}, u32[]{:S(2)}, u32[]{:S(2)}) collective-permute-start(f32[2,256,128]{2,1,0:T(8,128)S(1)} %get-tuple-element.14), channel_id=1, source_target_pairs={{1,0},{3,2},{5,4},{7,6},{9,8},{11,10},{13,12},{15,14},{17,16},{19,... | collective-permute-start | bytes 786440 | tf_op jit(solution)/shard_map/ppermute | solution.py:27
  99.1 3.1 %copy-start = (f32[8,2,8,8,128]{4,3,0,2,1:T(8,128)S(1)}, f32[8,2,8,8,128]{4,3,0,2,1:T(8,128)}, u32[]{:S(2)}) copy-start(f32[8,2,8,8,128]{4,3,0,2,1:T(8,128)} %copy.95) | copy-start | bytes 1572868
  99.1 3.1 %copy-start.1 = (f32[8,2,8,8,128]{4,3,0,2,1:T(8,128)S(1)}, f32[8,2,8,8,128]{4,3,0,2,1:T(8,128)}, u32[]{:S(2)}) copy-start(f32[8,2,8,8,128]{4,3,0,2,1:T(8,128)} %copy.96) | copy-start | bytes 1572868
  99.1 3.1 %copy-start.2 = (f32[8,2,8,8,128]{4,3,0,2,1:T(8,128)S(1)}, f32[8,2,8,8,128]{4,3,0,2,1:T(8,128)}, u32[]{:S(2)}) copy-start(f32[8,2,8,8,128]{4,3,0,2,1:T(8,128)} %copy.97) | copy-start | bytes 1572868
  99.1 3.1 %copy-start.3 = (f32[1,256,2,256]{3,1,2,0:T(8,128)S(1)}, f32[1,256,2,256]{3,1,2,0:T(8,128)}, u32[]{:S(2)}) copy-start(f32[1,256,2,256]{3,1,2,0:T(8,128)} %get-tuple-element.15) | copy-start | bytes 1572868
  99.2 3.1 %copy-start.4 = (f32[1,256,2,256]{3,1,2,0:T(8,128)S(1)}, f32[1,256,2,256]{3,1,2,0:T(8,128)}, u32[]{:S(2)}) copy-start(f32[1,256,2,256]{3,1,2,0:T(8,128)} %get-tuple-element.18) | copy-start | bytes 1572868
